TPU v7x, 32 devices: a whole 2x2x4 slice. The times are simulated.
32 devices in a mesh: comp: 2 (over core), gx: 4 (over y, x), gy: 4 (over z).
Axes of the slice: x: 2, y: 2, z: 4, core: 2. Of those that a mesh axis runs over, the one named last changes fastest.
Arguments:
- state: float32 [2, 8, 96, 3072], P('comp', None, 'gx', 'gy'), may hold values from -6 to 6
- response: float32 [2, 8, 3072], P('comp'), may hold values from -0.95 to 0
- diffusion: float32 [2, 96, 3072], P('comp', 'gx', 'gy'), may hold values from 0.02 to 0.24
- land_mask: int32 [96, 3072], P('gx', 'gy'), may hold values 0 or 1
- couple_src: int32 [2, 4, 4, 16, 128], P('comp', 'gx', 'gy'), may hold values from 0 to 18431
- couple_dst: int32 [2, 4, 4, 16, 128], P('comp', 'gx', 'gy'), may hold values from 0 to 18431
- couple_weight: float32 [2, 4, 4, 16, 128], P('comp', 'gx', 'gy'), may hold values from 0.1 to 1
- couple_count: int32 [2, 4, 4, 16], P('comp', 'gx', 'gy'), may hold values from 0 to 128, as said below
Outputs:
- final_state: float32 [2, 8, 96, 3072], P('comp', None, 'gx', 'gy')
Inputs may be any that keep to these rules, and one draw needn't show every extreme that they name: `couple_count`: at most 128 live slots per ordered device pair; every sending device has one pair with exactly 128.
All inputs are finite; a program needn't handle non-finite values. No bound on the sum of `land_mask` on one device may be relied on, other than what follows from the above.
Results may differ from a plain program's by a relative error of at most 0.0095.
Values may be sent and summed in bfloat16 or wider, within the bound.
A program may use at most 128 MiB of HBM per device.

v0:
```python
import math
import jax
import jax.numpy as jnp
from jax import lax
from jax.sharding import PartitionSpec as P

FC = 4


def extended(block, sides, width):
    for axis, dim in sides:
        count = lax.axis_size(axis)
        forward = [(i, i + 1) for i in range(count - 1)]
        backward = [(target, source) for source, target in forward]
        low = lax.ppermute(
            lax.slice_in_dim(block, block.shape[dim] - width, None, axis=dim), axis, forward
        )
        high = lax.ppermute(lax.slice_in_dim(block, 0, width, axis=dim), axis, backward)
        block = jnp.concatenate([low, block, high], axis=dim)
    return block


def partner(value, axis, stride):
    mask = 2**stride
    pairs = [(source, source ^ mask) for source in range(lax.axis_size(axis))]
    return lax.ppermute(value, axis, pairs)


def make_table(cols):
    rows_idx = jnp.arange(cols, dtype=jnp.int32)[:, None]
    wave_idx = jnp.arange(cols // 2, dtype=jnp.int32)[None, :]
    phase = rows_idx * wave_idx % cols
    angle = phase.astype(jnp.float32) * (2.0 * math.pi / cols)
    return jnp.concatenate([jnp.cos(angle), jnp.sin(angle)], axis=1).astype(jnp.bfloat16)


def back_transform(filtered, table_part):
    return lax.dot_general(
        filtered, table_part, (((1,), (1,)), ((), ())), preferred_element_type=jnp.float32
    )


def circle_increment(circles, resp_part, table, scale):
    count, rows_part, cols_all = circles.shape
    spec = jnp.dot(circles.reshape(-1, cols_all), table, preferred_element_type=jnp.float32)
    spec = spec.reshape(count, rows_part, cols_all)
    filtered = (spec * resp_part[:, None, :]).astype(jnp.bfloat16)
    incr = (back_transform(filtered.reshape(-1, cols_all), table) * scale).astype(jnp.bfloat16)
    return incr.reshape(count, rows_part, cols_all)


def diffuse(fields, rate):
    padded = extended(fields.astype(jnp.bfloat16), (("gx", 1),), 1).astype(fields.dtype)
    return fields + rate[None] * (padded[:, 2:] + padded[:, :-2] - 2.0 * fields)


def local(
    state, response, diffusion, land_mask, couple_src, couple_dst, couple_weight, couple_count
):
    levels, rows_dev, cols_dev = (state.shape[1], state.shape[2], state.shape[3])
    groups_x = lax.axis_size("gx")
    groups_y = lax.axis_size("gy")
    peers = groups_x * groups_y
    slots = couple_src.shape[4]
    cells = rows_dev * cols_dev
    cols_all = cols_dev * groups_y
    per_level = levels // groups_y
    section = lax.axis_index("comp")
    keep = jnp.where(section == 1, land_mask.astype(jnp.float32), jnp.float32(1.0))
    table = make_table(cols_all)
    scale = 2.0 / cols_all
    src_idx = couple_src.reshape(peers, slots)
    dst_idx = couple_dst.reshape(peers, slots)
    live = jnp.arange(slots, dtype=jnp.int32)[None, :] < couple_count.reshape(peers, 1)
    weights = jnp.where(live, couple_weight.reshape(peers, slots), jnp.float32(0.0))
    first_level = lax.axis_index("gy") * per_level
    resp_mine = lax.dynamic_slice_in_dim(response[0], first_level, per_level, 0)
    rate = diffusion[0]
    fields = state[0]
    surface = fields[:FC].reshape(FC, cells)
    outgoing = jnp.transpose(surface[:, src_idx] * weights[None], (1, 0, 2))
    crossed = partner(outgoing, "comp", 0)
    arrived = lax.all_to_all(crossed, ("gx", "gy"), split_axis=0, concat_axis=0, tiled=True)
    incoming = jnp.transpose(arrived, (1, 0, 2))
    surface = surface.at[:, dst_idx].add(incoming)
    surf = surface.reshape(FC, rows_dev, cols_dev)
    fields = jnp.concatenate([surf, fields[FC:]], axis=0)
    grid_bf = fields.astype(jnp.bfloat16)
    circles = lax.all_to_all(grid_bf, "gy", split_axis=0, concat_axis=2, tiled=True)
    incr = circle_increment(circles, resp_mine, table, scale)
    incr = lax.all_to_all(incr, "gy", split_axis=2, concat_axis=0, tiled=True)
    fields = fields + incr.astype(jnp.float32)
    fields = diffuse(fields, rate) * keep[None]
    return fields[None]


def solution(mesh):
    return jax.shard_map(
        local,
        mesh=mesh,
        in_specs=(
            P("comp", None, "gx", "gy"),
            P("comp", None, None),
            P("comp", "gx", "gy"),
            P("gx", "gy"),
            P("comp", "gx", "gy", None, None),
            P("comp", "gx", "gy", None, None),
            P("comp", "gx", "gy", None, None),
            P("comp", "gx", "gy", None),
        ),
        out_specs=P("comp", None, "gx", "gy"),
        check_vma=False,
    )
```

profile of v0, /device:TPU:4, one launch (start us, length us, event | category | flops | bytes accessed | tf_op | source)
XLA Modules:
  0.0 198.0 jit_solution(5701691548152781341)
XLA Ops:
  0.0 0.0 copy-start
  0.0 0.0 copy-start.2
  0.0 0.0 copy-start.3
  0.0 0.0 copy-start.5
  0.0 0.0 copy-start.4
  0.0 1.1 fusion.28
  1.2 0.0 copy-start.1
  1.2 5.6 %copy.20 = f32[1,4,24,768]{1,3,2,0:T(8,128)} copy(f32[1,4,24,768]{3,2,1,0:T(8,128)S(1)} %get-tuple-element.5) | data formatting | bytes 589824 | tf_op jit(solution)/shard_map/slice | solution.py:80
  6.8 0.0 copy-done.2
  6.8 9.1 %gather_fusion = f32[2048,4]{1,0:T(8,128)S(1)} fusion(f32[4,18432]{0,1:T(8,128)} %bitcast.55, s32[2048]{0:T(1024)S(1)} %fusion.25), kind=kCustom, calls=%fused_computation | custom fusion | bytes 73728 | tf_op jit(solution)/shard_map/gather | solution.py:81
  16.0 0.3 copy.21
  16.3 0.0 copy-done.3
  16.3 0.0 copy-done.5
  16.3 0.1 bitcast_select_fusion
  16.4 0.1 collective-permute-start
  16.5 1.2 collective-permute-done
  17.7 0.6 copy.22
  18.3 7.3 %all-to-all-start = ((f32[16,4,128]{2,1,0:T(4,128)}), f32[16,4,128]{2,1,0:T(4,128)S(1)}, u32[]{:S(2)}, u32[]{:S(2)}) async-start(f32[16,4,128]{2,1,0:T(4,128)} %copy.22), calls=%async_computation | async-start | bytes 65536 | tf_op jit(solution)/shard_map/all_to_all | solution.py:83
  25.6 0.0 copy-done.4
  25.6 6.1 %all-to-all-done = f32[16,4,128]{2,1,0:T(4,128)S(1)} async-done(((f32[16,4,128]{2,1,0:T(4,128)}), f32[16,4,128]{2,1,0:T(4,128)S(1)}, u32[]{:S(2)}, u32[]{:S(2)}) %all-to-all-start) | async-done | bytes 32800 | tf_op jit(solution)/shard_map/all_to_all | solution.py:83
  31.7 0.4 copy.23
  32.0 17.6 %scatter_fusion = f32[4,18432]{0,1:T(8,128)} fusion(f32[4,18432]{0,1:T(8,128)} %bitcast.56, s32[2048]{0:T(1024)S(1)} %fusion.23, f32[2048,4]{1,0:T(8,128)S(1)} %copy.23), kind=kCustom, calls=%fused_computation.1 | custom fusion | flops 8192 | bytes 106496 | tf_op jit(solution)/shard_map/scatter-add | solution.py:85
  49.7 6.4 %copy.24 = f32[4,24,768]{2,1,0:T(8,128)S(1)} copy(f32[4,24,768]{0,2,1:T(8,128)} %bitcast.57) | data formatting | bytes 589824 | tf_op jit(solution)/shard_map/reshape | solution.py:86
  56.1 0.0 copy-done.1
  56.1 0.7 fusion.21
  56.8 3.5 %all-to-all-start.1 = ((bf16[8,24,768]{2,1,0:T(8,128)(2,1)}), bf16[8,24,768]{2,1,0:T(8,128)(2,1)S(1)}, u32[]{:S(2)}, u32[]{:S(2)}) async-start(bf16[8,24,768]{2,1,0:T(8,128)(2,1)} %fusion.21), calls=%async_computation.1 | async-start | bytes 589824 | tf_op jit(solution)/shard_map/all_to_all | solution.py:89
  60.3 79.5 %sine_convert_fusion = (bf16[3072,1536]{1,0:T(8,128)(2,1)}, bf16[3072,1536]{1,0:T(8,128)(2,1)}) fusion(), kind=kLoop, calls=%fused_computation.8 | loop fusion | flops 51904512 | bytes 18874368 | tf_op jit(solution)/shard_map/convert.4
  139.8 0.0 copy-done
  139.8 0.0 all-to-all-done.1
  139.8 0.2 copy.29
  140.0 0.2 dot_general.8
  140.2 8.2 %fusion.12 = bf16[2,24,3072]{2,1,0:T(8,128)(2,1)S(1)} fusion(bf16[2,24,3072]{2,1,0:T(8,128)(2,1)S(1)} %dot_general.8, bf16[3072,1536]{1,0:T(8,128)(2,1)} %get-tuple-element.9, bf16[3072,1536]{1,0:T(8,128)(2,1)} %get-tuple-element.10, f32[2,3072]{1,0:T(2,128)S(1)} %dynamic-slice_bitcast_fusion), kind=kOutput, calls=%fused_computation.17 | convolution fusion | flops 944013312 | bytes 19488768 | tf_op jit(solution)/shard_map/dot_general | solution.py:45
  148.4 9.6 %fusion.15 = bf16[48,3072]{1,0:T(8,128)(2,1)S(1)} fusion(bf16[48,3072]{1,0:T(8,128)(2,1)S(1)} %bitcast.67, bf16[3072,1536]{1,0:T(8,128)(2,1)} %get-tuple-element.9, bf16[3072,1536]{1,0:T(8,128)(2,1)} %get-tuple-element.10), kind=kOutput, calls=%fused_computation.18 | convolution fusion | flops 944013312 | bytes 19464192 | tf_op jit(solution)/shard_map/dot_general | solution.py:38
  158.1 1.9 copy.26
  160.0 2.6 %reshape.148 = bf16[4,2,18432]{2,1,0:T(2,128)(2,1)} reshape(bf16[3072,2,24]{2,1,0:T(2,128)(2,1)S(1)} %bitcast.58) | data formatting | bytes 589824
  162.6 5.0 %all-to-all-start.2 = ((bf16[4,2,18432]{2,1,0:T(2,128)(2,1)}), bf16[4,2,18432]{2,1,0:T(2,128)(2,1)S(1)}, u32[]{:S(2)}, u32[]{:S(2)}) async-start(bf16[4,2,18432]{2,1,0:T(2,128)(2,1)} %reshape.148), calls=%async_computation.2 | async-start | bytes 589824 | tf_op jit(solution)/shard_map/all_to_all | solution.py:91
  167.7 8.3 %all-to-all-done.2 = bf16[4,2,18432]{2,1,0:T(2,128)(2,1)S(1)} async-done(((bf16[4,2,18432]{2,1,0:T(2,128)(2,1)}), bf16[4,2,18432]{2,1,0:T(2,128)(2,1)S(1)}, u32[]{:S(2)}, u32[]{:S(2)}) %all-to-all-start.2) | async-done | bytes 294944 | tf_op jit(solution)/shard_map/all_to_all | solution.py:91
  176.0 3.1 %reshape.149 = bf16[3072,2,24]{2,1,0:T(2,128)(2,1)} reshape(bf16[4,2,18432]{2,1,0:T(2,128)(2,1)S(1)} %all-to-all-done.2) | data formatting | bytes 589824
  179.1 2.5 %convert_bitcast_fusion = f32[4,2,24,768]{2,1,3,0:T(2,128)S(1)} fusion(bf16[2,24,4,768]{1,0,3,2:T(2,128)(2,1)} %bitcast.59), kind=kLoop, calls=%fused_computation.19 | loop fusion | flops 147456 | bytes 884736 | tf_op jit(solution)/shard_map/convert_element_type | solution.py:92
  181.6 2.8 %copy.27 = f32[4,2,24,768]{3,2,1,0:T(8,128)} copy(f32[4,2,24,768]{2,1,3,0:T(2,128)S(1)} %convert_bitcast_fusion) | data formatting | bytes 1179648 | tf_op jit(solution)/shard_map/convert_element_type | solution.py:92
  184.4 1.2 fusion.22
  185.7 3.4 %collective-permute-start.2 = (bf16[8,1,768]{2,1,0:T(2,128)(2,1)S(1)}, bf16[8,1,768]{2,1,0:T(2,128)(2,1)S(1)}, u32[]{:S(2)}, u32[]{:S(2)}) collective-permute-start(bf16[8,1,768]{2,1,0:T(2,128)(2,1)S(1)} %get-tuple-element.8), channel_id=1, source_target_pairs={{4,0},{8,4},{12,8},{5,1},{9,5},{13,9},{6,2},{10,6},{14,10},{7,3},{... | collective-permute-start | bytes 36872 | tf_op jit(solution)/shard_map/ppermute | solution.py:18
  189.0 2.5 %collective-permute-start.1 = (bf16[8,1,768]{2,1,0:T(2,128)(2,1)S(1)}, bf16[8,1,768]{2,1,0:T(2,128)(2,1)S(1)}, u32[]{:S(2)}, u32[]{:S(2)}) collective-permute-start(bf16[8,1,768]{2,1,0:T(2,128)(2,1)S(1)} %get-tuple-element.7), channel_id=1, source_target_pairs={{0,4},{4,8},{8,12},{1,5},{5,9},{9,13},{2,6},{6,10},{10,14},{3,7},{... | collective-permute-start | bytes 36872 | tf_op jit(solution)/shard_map/ppermute | solution.py:15
  191.5 0.9 convert_select_fusion
  192.4 0.0 collective-permute-done.2
  192.4 3.2 %collective-permute-done.1 = bf16[8,1,768]{2,1,0:T(2,128)(2,1)S(1)} collective-permute-done((bf16[8,1,768]{2,1,0:T(2,128)(2,1)S(1)}, bf16[8,1,768]{2,1,0:T(2,128)(2,1)S(1)}, u32[]{:S(2)}, u32[]{:S(2)}) %collective-permute-start.1) | collective-permute-done | bytes 12320 | tf_op jit(solution)/shard_map/ppermute | solution.py:15
  195.7 0.1 maximum_convert_fusion
  195.8 2.2 %fusion.20 = f32[1,8,24,768]{3,2,1,0:T(8,128)} fusion(f32[8,26,768]{2,1,0:T(8,128)S(1)} %maximum_convert_fusion, f32[24,768]{1,0:T(8,128)S(1)} %convert_select_fusion, f32[24,768]{1,0:T(8,128)} %bitcast.65, f32[4,2,24,768]{3,2,1,0:T(8,128)} %copy.27, f32[4,24,768]{2,1,0:T(8,128)} %copy-done.1, f32[4,24,768]{2,1,0:T(8,128)S(1)} %copy.24), kind=kLoop, calls=%fused_computation.25 | loop fusion | flops 1179648 | bytes 3096576 | tf_op jit(solution)/shard_map/broadcast_in_dim | solution.py:94
  (5 shorter events, 0.1 us)
Async XLA Ops:
  0.0 139.8 %copy-start = (f32[1,8,3072]{2,1,0:T(8,128)S(1)}, f32[1,8,3072]{2,1,0:T(8,128)}, u32[]{:S(2)}) copy-start(f32[1,8,3072]{2,1,0:T(8,128)} %param.9) | copy-start | bytes 294916
  0.0 6.8 %copy-start.2 = (s32[1,1,1,16,128]{4,3,2,1,0:T(8,128)S(1)}, s32[1,1,1,16,128]{4,3,2,1,0:T(8,128)}, u32[]{:S(2)}) copy-start(s32[1,1,1,16,128]{4,3,2,1,0:T(8,128)} %param.12) | copy-start | bytes 24580
  0.0 16.3 %copy-start.3 = (f32[1,1,1,16,128]{4,3,2,1,0:T(8,128)S(1)}, f32[1,1,1,16,128]{4,3,2,1,0:T(8,128)}, u32[]{:S(2)}) copy-start(f32[1,1,1,16,128]{4,3,2,1,0:T(8,128)} %param.14) | copy-start | bytes 24580
  0.0 16.3 %copy-start.5 = (s32[1,1,1,16]{3,2,1,0:T(1,128)S(1)}, s32[1,1,1,16]{3,2,1,0:T(1,128)}, u32[]{:S(2)}) copy-start(s32[1,1,1,16]{3,2,1,0:T(1,128)} %param.15) | copy-start | bytes 196
  0.0 25.6 %copy-start.4 = (s32[1,1,1,16,128]{4,3,2,1,0:T(8,128)S(1)}, s32[1,1,1,16,128]{4,3,2,1,0:T(8,128)}, u32[]{:S(2)}) copy-start(s32[1,1,1,16,128]{4,3,2,1,0:T(8,128)} %param.13) | copy-start | bytes 24580
  1.2 54.9 %copy-start.1 = (f32[4,24,768]{2,1,0:T(8,128)}, f32[4,24,768]{2,1,0:T(8,128)S(1)}, u32[]{:S(2)}) copy-start(f32[4,24,768]{2,1,0:T(8,128)S(1)} %get-tuple-element.6) | copy-start | bytes 884740
  16.4 1.3 collective-permute-start
  18.3 13.4 %all-to-all-start = ((f32[16,4,128]{2,1,0:T(4,128)}), f32[16,4,128]{2,1,0:T(4,128)S(1)}, u32[]{:S(2)}, u32[]{:S(2)}) async-start(f32[16,4,128]{2,1,0:T(4,128)} %copy.22), calls=%async_computation | async-start | bytes 65536 | tf_op jit(solution)/shard_map/all_to_all | solution.py:83
  56.8 83.0 %all-to-all-start.1 = ((bf16[8,24,768]{2,1,0:T(8,128)(2,1)}), bf16[8,24,768]{2,1,0:T(8,128)(2,1)S(1)}, u32[]{:S(2)}, u32[]{:S(2)}) async-start(bf16[8,24,768]{2,1,0:T(8,128)(2,1)} %fusion.21), calls=%async_computation.1 | async-start | bytes 589824 | tf_op jit(solution)/shard_map/all_to_all | solution.py:89
  162.6 13.3 %all-to-all-start.2 = ((bf16[4,2,18432]{2,1,0:T(2,128)(2,1)}), bf16[4,2,18432]{2,1,0:T(2,128)(2,1)S(1)}, u32[]{:S(2)}, u32[]{:S(2)}) async-start(bf16[4,2,18432]{2,1,0:T(2,128)(2,1)} %reshape.148), calls=%async_computation.2 | async-start | bytes 589824 | tf_op jit(solution)/shard_map/all_to_all | solution.py:91
  185.7 6.8 %collective-permute-start.2 = (bf16[8,1,768]{2,1,0:T(2,128)(2,1)S(1)}, bf16[8,1,768]{2,1,0:T(2,128)(2,1)S(1)}, u32[]{:S(2)}, u32[]{:S(2)}) collective-permute-start(bf16[8,1,768]{2,1,0:T(2,128)(2,1)S(1)} %get-tuple-element.8), channel_id=1, source_target_pairs={{4,0},{8,4},{12,8},{5,1},{9,5},{13,9},{6,2},{10,6},{14,10},{7,3},{... | collective-permute-start | bytes 36872 | tf_op jit(solution)/shard_map/ppermute | solution.py:18
  189.0 6.6 %collective-permute-start.1 = (bf16[8,1,768]{2,1,0:T(2,128)(2,1)S(1)}, bf16[8,1,768]{2,1,0:T(2,128)(2,1)S(1)}, u32[]{:S(2)}, u32[]{:S(2)}) collective-permute-start(bf16[8,1,768]{2,1,0:T(2,128)(2,1)S(1)} %get-tuple-element.7), channel_id=1, source_target_pairs={{0,4},{4,8},{8,12},{1,5},{5,9},{9,13},{2,6},{6,10},{10,14},{3,7},{... | collective-permute-start | bytes 36872 | tf_op jit(solution)/shard_map/ppermute | solution.py:15
where the time goes:
time: 199 us; the launch traced here: 198 us
  other arithmetic  105 us (53%)
  local copies, waits for them, and re-layouts  34.5 us (17%)
  starting transfers between devices  21.7 us (11%)
  waiting for transfers between devices  18.8 us (9%)
  matrix products  17.8 us (9%)
    another operation x1, other arithmetic  79.5 us
    scatter-add x1, other arithmetic, local(): surface = surface.at[:, dst_idx].add(incoming)  17.6 us
    dot_general x1, matrix products, back_transform(): lax.dot_general(filtered, table_part, (((1,), (1,)), ((), ())), preferred...  9.63 us
    gather x2, local copies, waits for them, and re-layouts, local(): outgoing = jnp.transpose(surface[:, src_idx] * weights[None], (1, 0, 2))  9.47 us
    all_to_all x1, waiting for transfers between devices, local(): incr = lax.all_to_all(incr, 'gy', split_axis=2, concat_axis=0, tiled=True)  8.3 us
    dot_general x1, matrix products, circle_increment(): jnp.dot(circles.reshape(-1, cols_all), table, preferred_element_type=jnp....  8.22 us
    all_to_all x1, starting transfers between devices, local(): lax.all_to_all(crossed, ('gx', 'gy'), split_axis=0, concat_axis=0, tiled=...  7.28 us
    slice x2, local copies, waits for them, and re-layouts, local(): surface = fields[:FC].reshape(FC, cells)  6.78 us
  transfers between devices with their start and end apart: 6, of which 4 were waited for; matrix products, arithmetic and copies ran while one was open for 41% of the time, Pallas kernels for 0%

commit v1 on v0

--- a/solution.py
+++ b/solution.py
@@ -5,6 +5,18 @@
 from jax.sharding import PartitionSpec as P
 
 FC = 4
+
+
+def cut_along(x, dim, count):
+    shape = x.shape
+    blocks = x.reshape(*shape[:dim], count, shape[dim] // count, *shape[dim + 1 :])
+    return jnp.moveaxis(blocks, dim, 0)
+
+
+def in_order(parts, dim):
+    parts = jnp.moveaxis(parts, 0, dim)
+    lengths = parts.shape
+    return parts.reshape(*lengths[:dim], lengths[dim] * lengths[dim + 1], *lengths[dim + 2 :])
 
 
 def extended(block, sides, width):
@@ -88,7 +100,14 @@
     grid_bf = fields.astype(jnp.bfloat16)
     circles = lax.all_to_all(grid_bf, "gy", split_axis=0, concat_axis=2, tiled=True)
     incr = circle_increment(circles, resp_mine, table, scale)
-    incr = lax.all_to_all(incr, "gy", split_axis=2, concat_axis=0, tiled=True)
+    devices, index = (lax.axis_size("gy"), lax.axis_index("gy"))
+    blocks = cut_along(incr, 2, devices)
+    finished = [blocks[index]]
+    for lap in range(1, devices):
+        sent = blocks[index ^ lap]
+        finished.append(lax.ppermute(sent, "gy", [(i_2, i_2 ^ lap) for i_2 in range(devices)]))
+    blocks = jnp.stack(finished)[index ^ jnp.arange(devices)]
+    incr = in_order(blocks, 0)
     fields = fields + incr.astype(jnp.float32)
     fields = diffuse(fields, rate) * keep[None]
     return fields[None]

time: 199 us -> 187 us (0.940)
  local copies, waits for them, and re-layouts: 34.5 us -> 25.5 us
  other arithmetic: 105 us -> 99.5 us
  waiting for transfers between devices: 18.8 us -> 22.7 us
    all_to_all x1, waiting for transfers between devices: 0.01 us -> 9.16 us  [local(): lax.all_to_all(grid_bf, 'gy', split_axis=0, concat_axis=2, tiled=True)]
    all_to_all x1 -> x0, waiting for transfers between devices: 8.3 us -> none  [local(): incr = lax.all_to_all(incr, 'gy', split_axis=2, concat_axis=0, tiled=True)]
    unnamed x14 -> x18, local copies, waits for them, and re-layouts: 5.79 us -> 0.08 us
    all_to_all x1 -> x0, starting transfers between devices: 5.04 us -> none  [local(): incr = lax.all_to_all(incr, 'gy', split_axis=2, concat_axis=0, tiled=True)]
    ppermute x0 -> x3, starting transfers between devices: none -> 4.58 us  [local(): lax.ppermute(sent, 'gy', [(i_2, i_2 ^ lap) for i_2 in range(devices)])]
    ppermute x0 -> x3, waiting for transfers between devices: none -> 3.49 us  [local(): lax.ppermute(sent, 'gy', [(i_2, i_2 ^ lap) for i_2 in range(devices)])]
    convert_element_type x1 -> x0, local copies, waits for them, and re-layouts: 2.83 us -> none  [local(): fields = fields + incr.astype(jnp.float32)]
    convert_element_type x1 -> x0, other arithmetic: 2.49 us -> none  [local(): fields = fields + incr.astype(jnp.float32)]
  transfers between devices with their start and end apart: 6 -> 8, of which waited for: 4 -> 5; matrix products, arithmetic and copies ran while one was open for 41% -> 43% of each run, Pallas kernels for 0% -> 0%
where the time goes in v1:
time: 187 us
  other arithmetic  99.5 us (53%)
  local copies, waits for them, and re-layouts  25.5 us (14%)
  waiting for transfers between devices  22.7 us (12%)
  starting transfers between devices  21.2 us (11%)
  matrix products  17.9 us (10%)
    another operation x1, other arithmetic  79.6 us
    scatter-add x1, other arithmetic, local(): surface = surface.at[:, dst_idx].add(incoming)  17.8 us
    dot_general x1, matrix products, back_transform(): lax.dot_general(filtered, table_part, (((1,), (1,)), ((), ())), preferred...  9.66 us
    gather x2, local copies, waits for them, and re-layouts, local(): outgoing = jnp.transpose(surface[:, src_idx] * weights[None], (1, 0, 2))  9.54 us
    all_to_all x1, waiting for transfers between devices, local(): lax.all_to_all(grid_bf, 'gy', split_axis=0, concat_axis=2, tiled=True)  9.16 us
    dot_general x1, matrix products, circle_increment(): jnp.dot(circles.reshape(-1, cols_all), table, preferred_element_type=jnp....  8.21 us
    all_to_all x1, starting transfers between devices, local(): lax.all_to_all(crossed, ('gx', 'gy'), split_axis=0, concat_axis=0, tiled=...  7.28 us
    slice x2, local copies, waits for them, and re-layouts, local(): surface = fields[:FC].reshape(FC, cells)  6.74 us
  transfers between devices with their start and end apart: 8, of which 5 were waited for; matrix products, arithmetic and copies ran while one was open for 43% of the time, Pallas kernels for 0%

profile of v1, /device:TPU:4, one launch (start us, length us, event | category | flops | bytes accessed | tf_op | source)
XLA Modules:
  0.0 187.1 jit_solution(11120111845295750813)
XLA Ops:
  0.0 0.0 copy-start
  0.0 0.0 copy-start.6
  0.0 1.1 fusion.29
  1.1 5.6 %copy.28 = f32[1,4,24,768]{1,3,2,0:T(8,128)} copy(f32[1,4,24,768]{3,2,1,0:T(8,128)S(1)} %get-tuple-element.5) | data formatting | bytes 589824 | tf_op jit(solution)/shard_map/slice | solution.py:92
  6.8 0.0 copy-done.3
  6.8 9.2 %gather_fusion = f32[2048,4]{1,0:T(8,128)S(1)} fusion(f32[4,18432]{0,1:T(8,128)} %bitcast.63, s32[2048]{0:T(1024)S(1)} %fusion.25), kind=kCustom, calls=%fused_computation | custom fusion | bytes 73728 | tf_op jit(solution)/shard_map/gather | solution.py:93
  16.0 0.3 copy.29
  16.3 0.0 copy-done.4
  16.3 0.0 copy-done.6
  16.3 0.1 bitcast_select_fusion
  16.4 0.0 copy-start.5
  16.4 0.1 collective-permute-start
  16.5 79.6 %sine_convert_fusion = (bf16[3072,1536]{1,0:T(8,128)(2,1)}, bf16[3072,1536]{1,0:T(8,128)(2,1)}) fusion(), kind=kLoop, calls=%fused_computation.9 | loop fusion | flops 51904512 | bytes 18874368 | tf_op jit(solution)/shard_map/convert.2
  96.1 0.0 collective-permute-done
  96.1 0.6 copy.30
  96.7 7.3 %all-to-all-start = ((f32[16,4,128]{2,1,0:T(4,128)}), f32[16,4,128]{2,1,0:T(4,128)S(1)}, u32[]{:S(2)}, u32[]{:S(2)}) async-start(f32[16,4,128]{2,1,0:T(4,128)} %copy.30), calls=%async_computation | async-start | bytes 65536 | tf_op jit(solution)/shard_map/all_to_all | solution.py:95
  104.0 0.0 copy-done.5
  104.0 6.0 %all-to-all-done = f32[16,4,128]{2,1,0:T(4,128)S(1)} async-done(((f32[16,4,128]{2,1,0:T(4,128)}), f32[16,4,128]{2,1,0:T(4,128)S(1)}, u32[]{:S(2)}, u32[]{:S(2)}) %all-to-all-start) | async-done | bytes 32800 | tf_op jit(solution)/shard_map/all_to_all | solution.py:95
  110.1 0.4 copy.31
  110.4 17.8 %scatter_fusion = f32[4,18432]{0,1:T(8,128)} fusion(f32[4,18432]{0,1:T(8,128)} %bitcast.64, s32[2048]{0:T(1024)S(1)} %fusion.23, f32[2048,4]{1,0:T(8,128)S(1)} %copy.31), kind=kCustom, calls=%fused_computation.2 | custom fusion | flops 8192 | bytes 106496 | tf_op jit(solution)/shard_map/scatter-add | solution.py:97
  128.2 6.4 %copy.32 = f32[4,24,768]{2,1,0:T(8,128)S(1)} copy(f32[4,24,768]{0,2,1:T(8,128)} %bitcast.65) | data formatting | bytes 589824 | tf_op jit(solution)/shard_map/reshape | solution.py:98
  134.6 0.8 fusion.21
  135.3 3.5 %all-to-all-start.1 = ((bf16[8,24,768]{2,1,0:T(8,128)(2,1)}), bf16[8,24,768]{2,1,0:T(8,128)(2,1)S(1)}, u32[]{:S(2)}, u32[]{:S(2)}) async-start(bf16[8,24,768]{2,1,0:T(8,128)(2,1)} %fusion.21), calls=%async_computation.1 | async-start | bytes 589824 | tf_op jit(solution)/shard_map/all_to_all | solution.py:101
  138.8 0.0 copy-done
  138.8 9.2 %all-to-all-done.1 = bf16[8,24,768]{2,1,0:T(8,128)(2,1)S(1)} async-done(((bf16[8,24,768]{2,1,0:T(8,128)(2,1)}), bf16[8,24,768]{2,1,0:T(8,128)(2,1)S(1)}, u32[]{:S(2)}, u32[]{:S(2)}) %all-to-all-start.1) | async-done | bytes 294944 | tf_op jit(solution)/shard_map/all_to_all | solution.py:101
  148.0 0.2 copy.47
  148.1 0.2 dot_general.8
  148.3 8.2 %fusion.12 = bf16[2,24,3072]{2,1,0:T(8,128)(2,1)S(1)} fusion(bf16[2,24,3072]{2,1,0:T(8,128)(2,1)S(1)} %dot_general.8, bf16[3072,1536]{1,0:T(8,128)(2,1)} %get-tuple-element.13, bf16[3072,1536]{1,0:T(8,128)(2,1)} %get-tuple-element.14, f32[2,3072]{1,0:T(2,128)S(1)} %dynamic-slice_bitcast_fusion), kind=kOutput, calls=%fused_computation.18 | convolution fusion | flops 944013312 | bytes 19488768 | tf_op jit(solution)/shard_map/dot_general | solution.py:57
  156.6 0.0 copy-start.2
  156.6 0.0 copy-start.1
  156.6 9.7 %fusion.15 = bf16[48,3072]{1,0:T(8,128)(2,1)S(1)} fusion(bf16[48,3072]{1,0:T(8,128)(2,1)S(1)} %bitcast.79, bf16[3072,1536]{1,0:T(8,128)(2,1)} %get-tuple-element.13, bf16[3072,1536]{1,0:T(8,128)(2,1)} %get-tuple-element.14), kind=kOutput, calls=%fused_computation.19 | convolution fusion | flops 944013312 | bytes 19464192 | tf_op jit(solution)/shard_map/dot_general | solution.py:50
  166.3 0.2 reshape_reshape.3
  166.5 0.6 constant_dynamic-slice_fusion.3
  167.1 1.5 collective-permute-start.3
  168.7 0.1 collective-permute-start.2
  168.8 3.0 %collective-permute-start.1 = (bf16[2,24,768]{2,1,0:T(8,128)(2,1)S(1)}, bf16[2,24,768]{2,1,0:T(8,128)(2,1)S(1)}, u32[]{:S(2)}, u32[]{:S(2)}) collective-permute-start(bf16[2,24,768]{2,1,0:T(8,128)(2,1)S(1)} %bitcast.77), channel_id=1, source_target_pairs={{0,1},{1,0},{2,3},{3,2},{4,5},{5,4},{6,7},{7,6},{8,9},{9,8},{10,11... | collective-permute-start | bytes 221192 | tf_op jit(solution)/shard_map/ppermute | solution.py:108
  171.7 2.2 %collective-permute-done.3 = bf16[2,24,768]{2,1,0:T(8,128)(2,1)S(1)} collective-permute-done((bf16[2,24,768]{2,1,0:T(8,128)(2,1)S(1)}, bf16[2,24,768]{2,1,0:T(8,128)(2,1)S(1)}, u32[]{:S(2)}, u32[]{:S(2)}) %collective-permute-start.3) | collective-permute-done | bytes 73760 | tf_op jit(solution)/shard_map/ppermute | solution.py:108
  174.0 1.3 collective-permute-done.2
  175.2 0.0 collective-permute-done.1
  175.3 0.6 gather_fusion.1
  175.9 0.1 fusion.22
  176.0 3.3 %collective-permute-start.5 = (bf16[8,1,768]{2,1,0:T(2,128)(2,1)S(1)}, bf16[8,1,768]{2,1,0:T(2,128)(2,1)S(1)}, u32[]{:S(2)}, u32[]{:S(2)}) collective-permute-start(bf16[8,1,768]{2,1,0:T(2,128)(2,1)S(1)} %get-tuple-element.8), channel_id=1, source_target_pairs={{4,0},{8,4},{12,8},{5,1},{9,5},{13,9},{6,2},{10,6},{14,10},{7,3},{... | collective-permute-start | bytes 36872 | tf_op jit(solution)/shard_map/ppermute | solution.py:30
  179.3 2.6 %collective-permute-start.4 = (bf16[8,1,768]{2,1,0:T(2,128)(2,1)S(1)}, bf16[8,1,768]{2,1,0:T(2,128)(2,1)S(1)}, u32[]{:S(2)}, u32[]{:S(2)}) collective-permute-start(bf16[8,1,768]{2,1,0:T(2,128)(2,1)S(1)} %get-tuple-element.7), channel_id=1, source_target_pairs={{0,4},{4,8},{8,12},{1,5},{5,9},{9,13},{2,6},{6,10},{10,14},{3,7},{... | collective-permute-start | bytes 36872 | tf_op jit(solution)/shard_map/ppermute | solution.py:27
  181.8 0.0 copy-done.2
  181.9 0.0 collective-permute-done.5
  181.9 4.0 %collective-permute-done.4 = bf16[8,1,768]{2,1,0:T(2,128)(2,1)S(1)} collective-permute-done((bf16[8,1,768]{2,1,0:T(2,128)(2,1)S(1)}, bf16[8,1,768]{2,1,0:T(2,128)(2,1)S(1)}, u32[]{:S(2)}, u32[]{:S(2)}) %collective-permute-start.4) | collective-permute-done | bytes 12320 | tf_op jit(solution)/shard_map/ppermute | solution.py:27
  185.9 0.1 maximum_convert_fusion
  186.0 1.0 fusion.20
  (16 shorter events, 0.2 us)
Async XLA Ops:
  0.0 138.8 %copy-start = (f32[1,8,3072]{2,1,0:T(8,128)S(1)}, f32[1,8,3072]{2,1,0:T(8,128)}, u32[]{:S(2)}) copy-start(f32[1,8,3072]{2,1,0:T(8,128)} %param.9) | copy-start | bytes 294916
  0.0 6.8 %copy-start.3 = (s32[1,1,1,16,128]{4,3,2,1,0:T(8,128)S(1)}, s32[1,1,1,16,128]{4,3,2,1,0:T(8,128)}, u32[]{:S(2)}) copy-start(s32[1,1,1,16,128]{4,3,2,1,0:T(8,128)} %param.12) | copy-start | bytes 24580
  0.0 16.3 %copy-start.4 = (f32[1,1,1,16,128]{4,3,2,1,0:T(8,128)S(1)}, f32[1,1,1,16,128]{4,3,2,1,0:T(8,128)}, u32[]{:S(2)}) copy-start(f32[1,1,1,16,128]{4,3,2,1,0:T(8,128)} %param.14) | copy-start | bytes 24580
  0.0 16.3 %copy-start.6 = (s32[1,1,1,16]{3,2,1,0:T(1,128)S(1)}, s32[1,1,1,16]{3,2,1,0:T(1,128)}, u32[]{:S(2)}) copy-start(s32[1,1,1,16]{3,2,1,0:T(1,128)} %param.15) | copy-start | bytes 196
  16.4 87.6 %copy-start.5 = (s32[1,1,1,16,128]{4,3,2,1,0:T(8,128)S(1)}, s32[1,1,1,16,128]{4,3,2,1,0:T(8,128)}, u32[]{:S(2)}) copy-start(s32[1,1,1,16,128]{4,3,2,1,0:T(8,128)} %param.13) | copy-start | bytes 24580
  16.4 79.6 %collective-permute-start = (f32[16,4,128]{2,0,1:T(8,128)S(1)}, f32[16,4,128]{2,0,1:T(8,128)S(1)}, u32[]{:S(2)}, u32[]{:S(2)}) collective-permute-start(f32[16,4,128]{2,0,1:T(8,128)S(1)} %multiply_bitcast_fusion), channel_id=1, source_target_pairs={{0,16},{16,0},{1,17},{17,1},{2,18},{18,2},{3,19},{19,3},{4,20},{20... | collective-permute-start | bytes 98312 | tf_op jit(solution)/shard_map/ppermute | solution.py:38
  96.7 13.4 %all-to-all-start = ((f32[16,4,128]{2,1,0:T(4,128)}), f32[16,4,128]{2,1,0:T(4,128)S(1)}, u32[]{:S(2)}, u32[]{:S(2)}) async-start(f32[16,4,128]{2,1,0:T(4,128)} %copy.30), calls=%async_computation | async-start | bytes 65536 | tf_op jit(solution)/shard_map/all_to_all | solution.py:95
  135.3 12.7 %all-to-all-start.1 = ((bf16[8,24,768]{2,1,0:T(8,128)(2,1)}), bf16[8,24,768]{2,1,0:T(8,128)(2,1)S(1)}, u32[]{:S(2)}, u32[]{:S(2)}) async-start(bf16[8,24,768]{2,1,0:T(8,128)(2,1)} %fusion.21), calls=%async_computation.1 | async-start | bytes 589824 | tf_op jit(solution)/shard_map/all_to_all | solution.py:101
  156.6 25.3 %copy-start.2 = (s32[24,768]{1,0:T(8,128)S(1)}, s32[24,768]{1,0:T(8,128)}, u32[]{:S(2)}) copy-start(s32[24,768]{1,0:T(8,128)} %param.11) | copy-start | bytes 221188
  156.6 29.4 %copy-start.1 = (f32[1,24,768]{2,1,0:T(8,128)S(1)}, f32[1,24,768]{2,1,0:T(8,128)}, u32[]{:S(2)}) copy-start(f32[1,24,768]{2,1,0:T(8,128)} %param.10) | copy-start | bytes 221188
  167.1 6.8 %collective-permute-start.3 = (bf16[2,24,768]{2,1,0:T(8,128)(2,1)S(1)}, bf16[2,24,768]{2,1,0:T(8,128)(2,1)S(1)}, u32[]{:S(2)}, u32[]{:S(2)}) collective-permute-start(bf16[2,24,768]{2,1,0:T(8,128)(2,1)S(1)} %bitcast.75), channel_id=1, source_target_pairs={{0,3},{1,2},{2,1},{3,0},{4,7},{5,6},{6,5},{7,4},{8,11},{9,10},{10,... | collective-permute-start | bytes 221192 | tf_op jit(solution)/shard_map/ppermute | solution.py:108
  168.7 6.6 %collective-permute-start.2 = (bf16[2,24,768]{2,1,0:T(8,128)(2,1)S(1)}, bf16[2,24,768]{2,1,0:T(8,128)(2,1)S(1)}, u32[]{:S(2)}, u32[]{:S(2)}) collective-permute-start(bf16[2,24,768]{2,1,0:T(8,128)(2,1)S(1)} %bitcast.76), channel_id=1, source_target_pairs={{0,2},{1,3},{2,0},{3,1},{4,6},{5,7},{6,4},{7,5},{8,10},{9,11},{10,... | collective-permute-start | bytes 221192 | tf_op jit(solution)/shard_map/ppermute | solution.py:108
  168.8 6.5 %collective-permute-start.1 = (bf16[2,24,768]{2,1,0:T(8,128)(2,1)S(1)}, bf16[2,24,768]{2,1,0:T(8,128)(2,1)S(1)}, u32[]{:S(2)}, u32[]{:S(2)}) collective-permute-start(bf16[2,24,768]{2,1,0:T(8,128)(2,1)S(1)} %bitcast.77), channel_id=1, source_target_pairs={{0,1},{1,0},{2,3},{3,2},{4,5},{5,4},{6,7},{7,6},{8,9},{9,8},{10,11... | collective-permute-start | bytes 221192 | tf_op jit(solution)/shard_map/ppermute | solution.py:108
  176.0 5.9 %collective-permute-start.5 = (bf16[8,1,768]{2,1,0:T(2,128)(2,1)S(1)}, bf16[8,1,768]{2,1,0:T(2,128)(2,1)S(1)}, u32[]{:S(2)}, u32[]{:S(2)}) collective-permute-start(bf16[8,1,768]{2,1,0:T(2,128)(2,1)S(1)} %get-tuple-element.8), channel_id=1, source_target_pairs={{4,0},{8,4},{12,8},{5,1},{9,5},{13,9},{6,2},{10,6},{14,10},{7,3},{... | collective-permute-start | bytes 36872 | tf_op jit(solution)/shard_map/ppermute | solution.py:30
  179.3 6.6 %collective-permute-start.4 = (bf16[8,1,768]{2,1,0:T(2,128)(2,1)S(1)}, bf16[8,1,768]{2,1,0:T(2,128)(2,1)S(1)}, u32[]{:S(2)}, u32[]{:S(2)}) collective-permute-start(bf16[8,1,768]{2,1,0:T(2,128)(2,1)S(1)} %get-tuple-element.7), channel_id=1, source_target_pairs={{0,4},{4,8},{8,12},{1,5},{5,9},{9,13},{2,6},{6,10},{10,14},{3,7},{... | collective-permute-start | bytes 36872 | tf_op jit(solution)/shard_map/ppermute | solution.py:27
